TPU v7x, 256 devices: a whole 4x4x8 slice. The times are simulated.
256 devices in a mesh: feat: 8 (over y, core), dom: 32 (over z, x).
Axes of the slice: x: 4, y: 4, z: 8, core: 2. Of those that a mesh axis runs over, the one named last changes fastest.
Arguments:
- features: bfloat16 [8, 4096, 4096], P(None, 'dom', 'feat'), may hold values from -6 to 6
- w_one: bfloat16 [4096, 1024], P('feat'), may hold values from -0.09375 to 0.09375
- w_two: bfloat16 [1024, 512], replicated, may hold values from -0.25 to 0.25
- neighbor: int32 [8, 4096, 10], P('feat', 'dom'), may hold values from 0 to 383
- degree: int32 [8, 4096], P('feat', 'dom'), may hold values from 1 to 10
- send_rows: int32 [8, 1024, 8], P('feat', 'dom'), may hold values from 0 to 127
- grad_out: bfloat16 [8, 4096, 512], P('feat', 'dom'), may hold values from -6 to 6
Outputs:
- out_two: bfloat16 [8, 4096, 512], P('feat', 'dom')
- grad_one: float32 [4096, 1024], P('feat')
- grad_two: float32 [1024, 512], replicated
All inputs are finite; a program needn't handle non-finite values.
Results may differ from a plain program's by a relative error of at most 0.015.
Values may be sent and summed in bfloat16 or wider, within the bound.
No kernel may reach another device: no remote copies, remote signals or barrier semaphores. Data moves between devices by JAX's collectives and lax.ppermute only.
A program may use at most 64 MiB of HBM per device.

v0:
```python
import math
import jax
import jax.numpy as jnp
from jax import lax
from jax.sharding import PartitionSpec as P


def trade(buffer):
    return lax.all_to_all(buffer, "dom", split_axis=0, concat_axis=0, tiled=True)


def on_device(features, w_one, w_two, neighbor, degree, send_rows, grad_out):
    groups, nodes, cols = features.shape
    width = w_two.shape[1]
    nbrs = neighbor[0]
    degs = degree[0]
    sends = send_rows[0]
    parts = lax.axis_size("dom")
    fan = nbrs.shape[1]
    slots = jnp.arange(fan, dtype=jnp.int32)
    weight = (slots[None, :] < degs[:, None]).astype(jnp.float32) / degs[:, None].astype(
        jnp.float32
    )
    flat = features.reshape(groups * nodes, cols)

    def spread(values):
        boxes = values[sends]
        recv = trade(boxes)
        table = jnp.concatenate([values, recv.reshape(-1, values.shape[1])], axis=0)
        gathered = table[nbrs]
        return jnp.sum(gathered.astype(jnp.float32) * weight[..., None], axis=1)

    def gather_back(grads):
        span = grads.shape[1]
        terms = (weight[..., None] * grads[:, None, :]).reshape(-1, span)
        table = jnp.zeros((nodes + sends.size, span), jnp.float32).at[nbrs.reshape(-1)].add(terms)
        local = table[:nodes]
        outgoing = table[nodes:].astype(jnp.bfloat16).reshape(parts, sends.shape[1], span)
        returned = trade(outgoing)
        home = (
            jnp.zeros((nodes, span), jnp.float32)
            .at[sends.reshape(-1)]
            .add(returned.reshape(-1, span).astype(jnp.float32))
        )
        return local + home

    rows = flat
    proj = lax.psum_scatter(
        jnp.dot(rows, w_one, preferred_element_type=jnp.float32),
        "feat",
        scatter_dimension=0,
        tiled=True,
    )
    p_self = proj[:, :width]
    p_near = proj[:, width:].astype(jnp.bfloat16)
    pre = p_self + spread(p_near)
    hidden = (pre * jax.nn.sigmoid(pre)).astype(jnp.bfloat16)
    agg = spread(hidden).astype(jnp.bfloat16)
    joined = jnp.concatenate([hidden, agg], axis=-1)
    out = jnp.dot(joined, w_two, preferred_element_type=jnp.float32).astype(jnp.bfloat16)
    grads = grad_out[0]
    two_sum = lax.dot_general(
        joined, grads, (((0,), (0,)), ((), ())), preferred_element_type=jnp.float32
    )
    dcat = lax.dot_general(
        grads, w_two, (((1,), (1,)), ((), ())), preferred_element_type=jnp.float32
    )
    d_hidden = dcat[:, :width] + gather_back(dcat[:, width:])
    sig = jax.nn.sigmoid(pre)
    d_pre = d_hidden * sig * (1.0 + pre * (1.0 - sig))
    d_near = gather_back(d_pre)
    d_proj = jnp.concatenate([d_pre, d_near], axis=-1).astype(jnp.bfloat16)
    rows = flat
    one_sum = lax.dot_general(
        rows,
        lax.all_gather(d_proj, "feat", axis=0, tiled=True),
        (((0,), (0,)), ((), ())),
        preferred_element_type=jnp.float32,
    )
    one_sum = lax.psum(one_sum.astype(jnp.bfloat16), "dom").astype(jnp.float32)
    two_sum = lax.psum(two_sum, ("feat", "dom"))
    scale = 1.0 / math.sqrt(groups * nodes * parts)
    return (out[None], one_sum * scale, two_sum * scale)


def solution(mesh):
    in_specs = (
        P(None, "dom", "feat"),
        P("feat", None),
        P(),
        P("feat", "dom", None),
        P("feat", "dom"),
        P("feat", "dom", None),
        P("feat", "dom", None),
    )
    out_specs = (P("feat", "dom", None), P("feat", None), P())
    return jax.shard_map(
        on_device, mesh=mesh, in_specs=in_specs, out_specs=out_specs, check_vma=False
    )
```

profile of v0, /device:TPU:8, one launch (start us, length us, event | category | flops | bytes accessed | tf_op | source)
XLA Modules:
  0.0 582.7 jit_solution(4482622993260259353)
XLA Ops:
  7.2 1.2 copy-done
  8.4 4.4 fusion.26
  14.5 2.5 mul.73
  17.0 4.5 mul.74
  21.9 13.1 %scatter_custom_fusion = f32[384,512]{1,0:T(8,128)S(1)} fusion(s32[1280]{0:T(1024)S(1)} %fusion.22, f32[1280,512]{1,0:T(8,128)} %mul.74, f32[1280]{0:T(1024)S(1)} %div.23, f32[]{:T(128)} %constant.9.clone.1), kind=kCustom, calls=%fused_computation.12 | custom fusion | flops 1310720 | bytes 3416068 | tf_op jit(solution)/shard_map/scatter-add | solution.py:36
  35.7 11.3 %all-to-all-start.2 = ((bf16[32,8,512]{2,1,0:T(8,128)(2,1)}), bf16[32,8,512]{2,1,0:T(8,128)(2,1)S(1)}, u32[]{:S(2)}, u32[]{:S(2)}) async-start(bf16[32,8,512]{2,1,0:T(8,128)(2,1)} %fusion.14), calls=%async_computation.3 | async-start | bytes 524288 | tf_op jit(solution)/shard_map/all_to_all | solution.py:9
  47.5 5.2 reduce-scatter.2.cloned.1.call-done
  53.7 1.9 gather_fusion
  55.5 4.2 all-to-all-done.2
  59.7 5.7 all-to-all-start
  65.6 2.4 scatter_custom_fusion.1
  68.0 10.6 %all-to-all-done = bf16[32,8,512]{2,1,0:T(8,128)(2,1)S(1)} async-done(((bf16[32,8,512]{2,1,0:T(8,128)(2,1)}), bf16[32,8,512]{2,1,0:T(8,128)(2,1)S(1)}, u32[]{:S(2)}, u32[]{:S(2)}) %all-to-all-start) | async-done | bytes 262176 | tf_op jit(solution)/shard_map/all_to_all | solution.py:9
  78.7 4.1 gather_fusion.1
  82.8 2.1 reshape.277
  84.9 3.2 multiply_reduce_fusion.1
  88.3 2.5 mul.79
  90.8 4.5 mul.80
  95.3 13.1 %scatter_custom_fusion.2 = f32[384,512]{1,0:T(8,128)S(1)} fusion(s32[1280]{0:T(1024)S(1)} %fusion.22, f32[1280,512]{1,0:T(8,128)} %mul.80, f32[1280]{0:T(1024)S(1)} %div.23, f32[]{:T(128)} %constant.9.clone.1), kind=kCustom, calls=%fused_computation.10 | custom fusion | flops 1310720 | bytes 3416068 | tf_op jit(solution)/shard_map/scatter-add | solution.py:36
  109.1 3.9 all-to-all-start.3
  113.0 12.2 %all-to-all-done.3 = bf16[32,8,512]{2,1,0:T(8,128)(2,1)S(1)} async-done(((bf16[32,8,512]{2,1,0:T(8,128)(2,1)}), bf16[32,8,512]{2,1,0:T(8,128)(2,1)S(1)}, u32[]{:S(2)}, u32[]{:S(2)}) %all-to-all-start.3) | async-done | bytes 262176 | tf_op jit(solution)/shard_map/all_to_all | solution.py:9
  125.3 2.2 scatter_custom_fusion.3
  129.5 15.7 %all_to_all.20 = bf16[32,8,512]{2,1,0:T(8,128)(2,1)S(1)} all-to-all(bf16[32,8,512]{2,1,0:T(8,128)(2,1)S(1)} %bitcast.50), channel_id=1, replica_groups=mesh['feat'=8,'dom'=32] {'dom'}, dimensions={0} | all-to-all | bytes 524288 | tf_op jit(solution)/shard_map/all_to_all | solution.py:9
  145.3 4.1 gather_fusion.3
  149.4 2.1 reshape.278
  151.6 3.2 multiply_reduce_fusion
  154.8 1.8 fusion.18
  156.7 3.9 fusion.4
  161.6 259.2 %all-reduce.5.cloned.1.call-done = f32[1024,512]{1,0:T(8,128)} async-done(((f32[1024,512]{1,0:T(8,128)}), f32[1024,512]{1,0:T(8,128)}) %all-reduce.5.cloned.1.call-update) | async-done | bytes 2097168 | tf_op jit(solution)/shard_map/psum | solution.py:81
  420.8 3.2 broadcast_multiply_fusion
  423.9 148.9 %all-reduce.3.cloned.1.call-done = bf16[512,1024]{0,1:T(8,128)(2,1)} async-done(((bf16[512,1024]{0,1:T(8,128)(2,1)}), bf16[512,1024]{0,1:T(8,128)(2,1)}) %all-reduce.3.cloned.1.call-update) | async-done | bytes 1048592 | tf_op jit(solution)/shard_map/psum | solution.py:80
  572.8 1.5 convert_multiply_fusion
  574.4 1.8 copy.15
  (57 shorter events, 8.4 us)
Async XLA Ops:
  7.2 1.2 copy-start
  7.2 45.5 %reduce-scatter.2.cloned.1.call-start = ((), (), s32[]{:S(2)}) async-start(), calls=%async_computation.5 | async-start | bytes 4718592 | tf_op jit(solution)/shard_map/reduce_scatter | solution.py:48
  12.8 0.7 copy-start.6
  12.8 1.2 copy-start.1
  12.8 1.2 copy-start.3
  17.0 4.5 copy-start.8
  21.6 25.4 %copy-start.7 = (s32[1,32,8]{1,2,0:T(8,128)S(1)}, s32[1,32,8]{1,2,0:T(8,128)}, u32[]{:S(2)}) copy-start(s32[1,32,8]{1,2,0:T(8,128)} %param.12) | copy-start | bytes 3076
  35.7 24.0 %all-to-all-start.2 = ((bf16[32,8,512]{2,1,0:T(8,128)(2,1)}), bf16[32,8,512]{2,1,0:T(8,128)(2,1)S(1)}, u32[]{:S(2)}, u32[]{:S(2)}) async-start(bf16[32,8,512]{2,1,0:T(8,128)(2,1)} %fusion.14), calls=%async_computation.3 | async-start | bytes 524288 | tf_op jit(solution)/shard_map/all_to_all | solution.py:9
  59.7 18.9 %all-to-all-start = ((bf16[32,8,512]{2,1,0:T(8,128)(2,1)}), bf16[32,8,512]{2,1,0:T(8,128)(2,1)S(1)}, u32[]{:S(2)}, u32[]{:S(2)}) async-start(bf16[32,8,512]{2,1,0:T(8,128)(2,1)} %bitcast.2), calls=%async_computation.1 | async-start | bytes 524288 | tf_op jit(solution)/shard_map/all_to_all | solution.py:9
  84.9 3.3 copy-start.5
  109.1 16.2 %all-to-all-start.3 = ((bf16[32,8,512]{2,1,0:T(8,128)(2,1)}), bf16[32,8,512]{2,1,0:T(8,128)(2,1)S(1)}, u32[]{:S(2)}, u32[]{:S(2)}) async-start(bf16[32,8,512]{2,1,0:T(8,128)(2,1)} %fusion.15), calls=%async_computation.4 | async-start | bytes 524288 | tf_op jit(solution)/shard_map/all_to_all | solution.py:9
  113.0 43.7 %all-gather.2.cloned.1.call-start = ((), (), s32[]{:S(2)}) async-start(), calls=%async_computation.6 | async-start | bytes 2359296 | tf_op jit(solution)/shard_map/all_gather | solution.py:76
  128.3 292.5 %all-reduce.5.cloned.1.call-start = ((), (), s32[]{:S(2)}) async-start(), calls=%async_computation.8 | async-start | bytes 4194304 | tf_op jit(solution)/shard_map/psum | solution.py:81
  151.6 3.2 copy-start.4
  156.6 4.0 copy-start.2
  156.6 416.2 %all-reduce.3.cloned.1.call-start = ((), (), s32[]{:S(2)}) async-start(), calls=%async_computation.7 | async-start | bytes 2097152 | tf_op jit(solution)/shard_map/psum | solution.py:80
Sparse Core Ops, SparseCore 0:
  12.9 39.6 reduce-scatter.1
  128.4 23.6 all-gather.1
  158.1 262.6 all-reduce.4
  424.7 148.1 all-reduce.2
where the time goes:
time: 583 us
  waiting for transfers between devices  440 us (75%)
  other arithmetic  43.1 us (7%)
  local copies, waits for them, and re-layouts  36.9 us (6%)
  starting transfers between devices  21 us (4%)
  blocking collectives  15.7 us (3%)
  between operations  14.1 us (2%)
  matrix products  11.5 us (2%)
    psum x1, waiting for transfers between devices, on_device(): two_sum = lax.psum(two_sum, ('feat', 'dom'))  259 us
    psum x1, waiting for transfers between devices, on_device(): one_sum = lax.psum(one_sum.astype(jnp.bfloat16), 'dom').astype(jnp.float32)  149 us
    all_to_all x3, waiting for transfers between devices, trade(): lax.all_to_all(buffer, 'dom', split_axis=0, concat_axis=0, tiled=True)  27 us
    scatter-add x2, other arithmetic, gather_back(): jnp.zeros((nodes + sends.size, span), jnp.float32).at[nbrs.reshape(-1)]  26.1 us
    all_to_all x3, starting transfers between devices, trade(): lax.all_to_all(buffer, 'dom', split_axis=0, concat_axis=0, tiled=True)  20.8 us
    all_to_all x1, blocking collectives, trade(): lax.all_to_all(buffer, 'dom', split_axis=0, concat_axis=0, tiled=True)  15.7 us
    mul x4, local copies, waits for them, and re-layouts, gather_back(): terms = (weight[..., None] * grads[:, None, :]).reshape(-1, span)  14 us
  transfers between devices with their start and end apart: 7, of which 6 were waited for; matrix products, arithmetic and copies ran while one was open for 8% of the time, Pallas kernels for 0%

commit v1 on v0

--- a/solution.py
+++ b/solution.py
@@ -3,6 +3,10 @@
 import jax.numpy as jnp
 from jax import lax
 from jax.sharding import PartitionSpec as P
+
+
+def _remake_field(sheet):
+    return jax.lax.psum(jax.lax.psum(sheet, "dom"), "feat")
 
 
 def trade(buffer):
@@ -78,7 +82,7 @@
         preferred_element_type=jnp.float32,
     )
     one_sum = lax.psum(one_sum.astype(jnp.bfloat16), "dom").astype(jnp.float32)
-    two_sum = lax.psum(two_sum, ("feat", "dom"))
+    two_sum = _remake_field(two_sum)
     scale = 1.0 / math.sqrt(groups * nodes * parts)
     return (out[None], one_sum * scale, two_sum * scale)
 

time: 583 us -> 537 us (0.921)
  waiting for transfers between devices: 440 us -> 393 us
    psum x1 -> x2, waiting for transfers between devices: 259 us -> 179 us  [_remake_field(): return jax.lax.psum(jax.lax.psum(sheet, 'dom'), 'feat')]
    all_gather x1, waiting for transfers between devices: 0.02 us -> 26.2 us  [on_device(): lax.all_gather(d_proj, 'feat', axis=0, tiled=True)]
  transfers between devices with their start and end apart: 7 -> 8, of which waited for: 6 -> 8; matrix products, arithmetic and copies ran while one was open for 8% -> 11% of each run, Pallas kernels for 0% -> 0%
where the time goes in v1:
time: 537 us
  waiting for transfers between devices  393 us (73%)
  other arithmetic  43.9 us (8%)
  local copies, waits for them, and re-layouts  36.8 us (7%)
  starting transfers between devices  21 us (4%)
  blocking collectives  16 us (3%)
  between operations  14.1 us (3%)
  matrix products  11.5 us (2%)
    psum x2, waiting for transfers between devices, _remake_field(): return jax.lax.psum(jax.lax.psum(sheet, 'dom'), 'feat')  179 us
    psum x1, waiting for transfers between devices, on_device(): one_sum = lax.psum(one_sum.astype(jnp.bfloat16), 'dom').astype(jnp.float32)  152 us
    all_to_all x3, waiting for transfers between devices, trade(): lax.all_to_all(buffer, 'dom', split_axis=0, concat_axis=0, tiled=True)  30 us
    scatter-add x2, other arithmetic, gather_back(): jnp.zeros((nodes + sends.size, span), jnp.float32).at[nbrs.reshape(-1)]  26.3 us
    all_gather x1, waiting for transfers between devices, on_device(): lax.all_gather(d_proj, 'feat', axis=0, tiled=True)  26.2 us
    all_to_all x3, starting transfers between devices, trade(): lax.all_to_all(buffer, 'dom', split_axis=0, concat_axis=0, tiled=True)  20.8 us
    all_to_all x1, blocking collectives, trade(): lax.all_to_all(buffer, 'dom', split_axis=0, concat_axis=0, tiled=True)  16 us
    mul x4, local copies, waits for them, and re-layouts, gather_back(): terms = (weight[..., None] * grads[:, None, :]).reshape(-1, span)  14 us
  transfers between devices with their start and end apart: 8, of which 8 were waited for; matrix products, arithmetic and copies ran while one was open for 11% of the time, Pallas kernels for 0%

profile of v1, /device:TPU:8, one launch (start us, length us, event | category | flops | bytes accessed | tf_op | source)
XLA Modules:
  0.0 536.5 jit_solution(1468334069499661558)
XLA Ops:
  8.4 4.4 fusion.26
  14.5 2.5 mul.73
  17.0 4.5 mul.74
  21.9 13.1 %scatter_custom_fusion = f32[384,512]{1,0:T(8,128)S(1)} fusion(s32[1280]{0:T(1024)S(1)} %fusion.22, f32[1280,512]{1,0:T(8,128)} %mul.74, f32[1280]{0:T(1024)S(1)} %div.23, f32[]{:T(128)} %constant.9.clone.1), kind=kCustom, calls=%fused_computation.12 | custom fusion | flops 1310720 | bytes 3416068 | tf_op jit(solution)/shard_map/scatter-add | solution.py:40
  35.7 11.3 %all-to-all-start.2 = ((bf16[32,8,512]{2,1,0:T(8,128)(2,1)}), bf16[32,8,512]{2,1,0:T(8,128)(2,1)S(1)}, u32[]{:S(2)}, u32[]{:S(2)}) async-start(bf16[32,8,512]{2,1,0:T(8,128)(2,1)} %fusion.14), calls=%async_computation.3 | async-start | bytes 524288 | tf_op jit(solution)/shard_map/all_to_all | solution.py:13
  47.5 5.2 reduce-scatter.2.cloned.1.call-done
  53.7 1.9 gather_fusion
  55.5 4.2 all-to-all-done.2
  59.7 5.7 %all-to-all-start = ((bf16[32,8,512]{2,1,0:T(8,128)(2,1)}), bf16[32,8,512]{2,1,0:T(8,128)(2,1)S(1)}, u32[]{:S(2)}, u32[]{:S(2)}) async-start(bf16[32,8,512]{2,1,0:T(8,128)(2,1)} %bitcast.2), calls=%async_computation.1 | async-start | bytes 524288 | tf_op jit(solution)/shard_map/all_to_all | solution.py:13
  65.6 2.4 scatter_custom_fusion.1
  68.1 10.5 %all-to-all-done = bf16[32,8,512]{2,1,0:T(8,128)(2,1)S(1)} async-done(((bf16[32,8,512]{2,1,0:T(8,128)(2,1)}), bf16[32,8,512]{2,1,0:T(8,128)(2,1)S(1)}, u32[]{:S(2)}, u32[]{:S(2)}) %all-to-all-start) | async-done | bytes 262176 | tf_op jit(solution)/shard_map/all_to_all | solution.py:13
  78.7 4.1 gather_fusion.1
  82.8 2.1 reshape.277
  84.9 3.2 multiply_reduce_fusion.1
  90.1 16.0 %all_to_all.20 = bf16[32,8,512]{2,1,0:T(8,128)(2,1)S(1)} all-to-all(bf16[32,8,512]{2,1,0:T(8,128)(2,1)S(1)} %bitcast.50), channel_id=1, replica_groups=mesh['feat'=8,'dom'=32] {'dom'}, dimensions={0} | all-to-all | bytes 524288 | tf_op jit(solution)/shard_map/all_to_all | solution.py:13
  106.1 4.1 gather_fusion.3
  110.2 2.1 reshape.278
  112.3 3.2 multiply_reduce_fusion
  115.6 1.8 fusion.18
  117.4 2.5 mul.79
  119.8 4.5 mul.80
  124.4 13.2 %scatter_custom_fusion.2 = f32[384,512]{1,0:T(8,128)S(1)} fusion(s32[1280]{0:T(1024)S(1)} %fusion.22, f32[1280,512]{1,0:T(8,128)} %mul.80, f32[1280]{0:T(1024)S(1)} %div.23, f32[]{:T(128)} %constant.9.clone.1), kind=kCustom, calls=%fused_computation.10 | custom fusion | flops 1310720 | bytes 3416068 | tf_op jit(solution)/shard_map/scatter-add | solution.py:40
  138.3 3.9 all-to-all-start.3
  142.3 15.3 %all-to-all-done.3 = bf16[32,8,512]{2,1,0:T(8,128)(2,1)S(1)} async-done(((bf16[32,8,512]{2,1,0:T(8,128)(2,1)}), bf16[32,8,512]{2,1,0:T(8,128)(2,1)S(1)}, u32[]{:S(2)}, u32[]{:S(2)}) %all-to-all-start.3) | async-done | bytes 262176 | tf_op jit(solution)/shard_map/all_to_all | solution.py:13
  157.6 2.2 scatter_custom_fusion.3
  160.7 112.1 %all-reduce.6.cloned.1.call-done = f32[1024,512]{1,0:T(8,128)} async-done(((f32[1024,512]{1,0:T(8,128)}), f32[1024,512]{1,0:T(8,128)}) %all-reduce.6.cloned.1.call-update) | async-done | bytes 2097168 | tf_op jit(solution)/shard_map/psum | solution.py:9
  272.9 26.2 %all-gather.2.cloned.1.call-done = bf16[1024,1024]{1,0:T(8,128)(2,1)} async-done(((bf16[128,1024]{1,0:T(8,128)(2,1)}), bf16[1024,1024]{1,0:T(8,128)(2,1)}) %all-gather.2.cloned.1.call-update) | async-done | bytes 2097168 | tf_op jit(solution)/shard_map/all_gather | solution.py:80
  299.0 3.8 fusion.4
  303.9 67.1 %all-reduce.8.cloned.1.call-done = f32[1024,512]{1,0:T(8,128)} async-done(((f32[1024,512]{1,0:T(8,128)}), f32[1024,512]{1,0:T(8,128)}) %all-reduce.8.cloned.1.call-update) | async-done | bytes 2097168 | tf_op jit(solution)/shard_map/psum | solution.py:9
  371.0 3.2 broadcast_multiply_fusion
  374.2 152.5 %all-reduce.4.cloned.1.call-done = bf16[512,1024]{0,1:T(8,128)(2,1)} async-done(((bf16[512,1024]{0,1:T(8,128)(2,1)}), bf16[512,1024]{0,1:T(8,128)(2,1)}) %all-reduce.4.cloned.1.call-update) | async-done | bytes 1048592 | tf_op jit(solution)/shard_map/psum | solution.py:84
  528.2 1.8 copy.15
  (62 shorter events, 11.8 us)
Async XLA Ops:
  7.2 1.2 copy-start
  7.2 45.5 %reduce-scatter.2.cloned.1.call-start = ((), (), s32[]{:S(2)}) async-start(), calls=%async_computation.5 | async-start | bytes 4718592 | tf_op jit(solution)/shard_map/reduce_scatter | solution.py:52
  12.8 0.7 copy-start.7
  12.8 1.2 copy-start.1
  12.8 1.2 copy-start.4
  17.0 4.5 copy-start.9
  21.6 25.4 %copy-start.8 = (s32[1,32,8]{1,2,0:T(8,128)S(1)}, s32[1,32,8]{1,2,0:T(8,128)}, u32[]{:S(2)}) copy-start(s32[1,32,8]{1,2,0:T(8,128)} %param.12) | copy-start | bytes 3076
  35.7 24.0 %all-to-all-start.2 = ((bf16[32,8,512]{2,1,0:T(8,128)(2,1)}), bf16[32,8,512]{2,1,0:T(8,128)(2,1)S(1)}, u32[]{:S(2)}, u32[]{:S(2)}) async-start(bf16[32,8,512]{2,1,0:T(8,128)(2,1)} %fusion.14), calls=%async_computation.3 | async-start | bytes 524288 | tf_op jit(solution)/shard_map/all_to_all | solution.py:13
  59.7 18.9 %all-to-all-start = ((bf16[32,8,512]{2,1,0:T(8,128)(2,1)}), bf16[32,8,512]{2,1,0:T(8,128)(2,1)S(1)}, u32[]{:S(2)}, u32[]{:S(2)}) async-start(bf16[32,8,512]{2,1,0:T(8,128)(2,1)} %bitcast.2), calls=%async_computation.1 | async-start | bytes 524288 | tf_op jit(solution)/shard_map/all_to_all | solution.py:13
  65.4 207.4 %all-reduce.6.cloned.1.call-start = ((), (), s32[]{:S(2)}) async-start(), calls=%async_computation.8 | async-start | bytes 4194304 | tf_op jit(solution)/shard_map/psum | solution.py:9
  84.9 3.3 copy-start.6
  112.3 3.2 copy-start.5
  124.3 35.5 %copy-start.3 = (bf16[128,512]{1,0:T(8,128)(2,1)S(1)}, bf16[128,512]{1,0:T(8,128)(2,1)}, u32[]{:S(2)}) copy-start(bf16[128,512]{1,0:T(8,128)(2,1)} %get-tuple-element.9) | copy-start | bytes 393220
  138.3 19.3 %all-to-all-start.3 = ((bf16[32,8,512]{2,1,0:T(8,128)(2,1)}), bf16[32,8,512]{2,1,0:T(8,128)(2,1)S(1)}, u32[]{:S(2)}, u32[]{:S(2)}) async-start(bf16[32,8,512]{2,1,0:T(8,128)(2,1)} %fusion.15), calls=%async_computation.4 | async-start | bytes 524288 | tf_op jit(solution)/shard_map/all_to_all | solution.py:13
  142.2 156.8 %all-gather.2.cloned.1.call-start = ((), (), s32[]{:S(2)}) async-start(), calls=%async_computation.6 | async-start | bytes 2359296 | tf_op jit(solution)/shard_map/all_gather | solution.py:80
  160.6 210.4 %all-reduce.8.cloned.1.call-start = ((), (), s32[]{:S(2)}) async-start(), calls=%async_computation.9 | async-start | bytes 4194304 | tf_op jit(solution)/shard_map/psum | solution.py:9
  272.8 30.1 %copy-start.2 = (bf16[1024,512]{1,0:T(8,128)(2,1)S(1)}, bf16[1024,512]{1,0:T(8,128)(2,1)}, u32[]{:S(2)}) copy-start(bf16[1024,512]{1,0:T(8,128)(2,1)} %param.9) | copy-start | bytes 3145732
  272.8 253.8 %all-reduce.4.cloned.1.call-start = ((), (), s32[]{:S(2)}) async-start(), calls=%async_computation.7 | async-start | bytes 2097152 | tf_op jit(solution)/shard_map/psum | solution.py:84
Sparse Core Ops, SparseCore 0:
  12.9 39.6 reduce-scatter.1
  117.5 155.2 all-reduce.5
  275.4 23.6 all-gather.1
  301.4 69.5 all-reduce.7
  375.3 151.3 all-reduce.3
